TPU v7x, 32 devices: a whole 2x2x4 slice. The times are simulated.
32 devices in a mesh: dp: 16 (over z, x, core), shard: 2 (over y).
Axes of the slice: x: 2, y: 2, z: 4, core: 2. Of those that a mesh axis runs over, the one named last changes fastest.
Arguments:
- tokens: bfloat16 [4096, 1088], P(('dp', 'shard')), may hold values from -6 to 6
- seq_ends: int32 [32, 3], P(('dp', 'shard')), may hold values from 0 to 128, as said below
- attn_weight: bfloat16 [1, 4352, 1088], P(None, ('dp', 'shard'))
- up_weight: bfloat16 [1, 4352, 1088], P(None, ('dp', 'shard')), may hold values from -0.1875 to 0.1875
- down_weight: bfloat16 [1, 4352, 1088], P(None, ('dp', 'shard')), may hold values from -0.09375 to 0.09375
- vectors: bfloat16 [1, 13056], P(None, ('dp', 'shard'))
- cotangent: bfloat16 [4096, 1088], P(('dp', 'shard')), may hold values from -6 to 6
Outputs:
- output: bfloat16 [4096, 1088], P(('dp', 'shard'))
- grad_tokens: float32 [4096, 1088], P(('dp', 'shard'))
- grad_attn: float32 [1, 4352, 1088], P(None, ('dp', 'shard'))
- grad_up: float32 [1, 4352, 1088], P(None, ('dp', 'shard'))
- grad_down: float32 [1, 4352, 1088], P(None, ('dp', 'shard'))
- grad_vectors: float32 [1, 13056], P(None, ('dp', 'shard'))
Inputs may be any that keep to these rules, and one draw needn't show every extreme that they name: `seq_ends`: each row lists non-decreasing end offsets of the sequences packed into one device's 128 slots; slots from the row's last end onward form one more segment.
All inputs are finite; a program needn't handle non-finite values.
Results may differ from a plain program's by a relative error of at most 0.0089.
Values may be sent and summed in bfloat16 or wider, within the bound.
A program may use at most 192 MiB of HBM per device.

v0:
```python
import jax
import jax.numpy as jnp
from jax import lax
from jax.sharding import PartitionSpec as P

HEAD_DIM = 64
EPS = 1e-05


def layer_norm(values, gain, shift):
    average = jnp.mean(values, axis=-1, keepdims=True)
    centred = values - average
    variance = jnp.mean(centred * centred, axis=-1, keepdims=True)
    return centred * lax.rsqrt(variance + EPS) * gain + shift


def gelu_tanh(values):
    return (
        0.5
        * values
        * (1.0 + jnp.tanh(0.7978845608028654 * (values + 0.044715 * values * values * values)))
    )


def contract_last(left, right):
    return lax.dot_general(
        left, right, (((1,), (1,)), ((), ())), preferred_element_type=jnp.float32
    )


def contract_first(left, right):
    return lax.dot_general(
        left, right, (((0,), (0,)), ((), ())), preferred_element_type=jnp.float32
    )


def head_product(form, left, right):
    return jnp.einsum(form, left, right, preferred_element_type=jnp.float32)


def causal_mask(ends_row, slot_count):
    positions = jnp.arange(slot_count, dtype=jnp.int32)
    segment = jnp.sum((ends_row[None, :] <= positions[:, None]).astype(jnp.int32), axis=1)
    return (segment[:, None] == segment[None, :]) & (positions[None, :] <= positions[:, None])


def split_vectors(vectors, model_width):
    vector_f32 = vectors.astype(jnp.float32)
    parts_list = [
        vector_f32[slot_idx * model_width : (slot_idx + 1) * model_width] for slot_idx in range(8)
    ]
    return parts_list + [vector_f32[8 * model_width :]]


def forward_layer(hidden, params, allowed):
    attn_part, up_part, down_part, vector_part = params
    model_width = attn_part.shape[1]
    head_count = model_width // HEAD_DIM
    row_count = hidden.shape[0]
    (
        gain_one,
        shift_one,
        query_bias,
        value_bias,
        out_bias,
        gain_two,
        shift_two,
        down_bias,
        up_bias,
    ) = split_vectors(vector_part, model_width)
    normed_one = layer_norm(hidden, gain_one, shift_one).astype(jnp.bfloat16)
    projected = contract_last(normed_one, attn_part[: 3 * model_width])
    query_heads = (
        ((projected[:, :model_width] + query_bias) * HEAD_DIM ** (-0.5))
        .astype(jnp.bfloat16)
        .reshape(row_count, head_count, HEAD_DIM)
    )
    key_heads = (
        projected[:, model_width : 2 * model_width]
        .astype(jnp.bfloat16)
        .reshape(row_count, head_count, HEAD_DIM)
    )
    value_heads = (
        (projected[:, 2 * model_width :] + value_bias)
        .astype(jnp.bfloat16)
        .reshape(row_count, head_count, HEAD_DIM)
    )
    scores = jnp.where(allowed[None], head_product("qhc,khc->hqk", query_heads, key_heads), -1e30)
    log_total = jnp.log(jnp.sum(jnp.exp(scores), axis=-1))
    weights = jnp.exp(scores - log_total[..., None]).astype(jnp.bfloat16)
    context = (
        head_product("hqk,khc->qhc", weights, value_heads)
        .reshape(row_count, model_width)
        .astype(jnp.bfloat16)
    )
    after_attn = (
        hidden
        + jnp.dot(context, attn_part[3 * model_width :], preferred_element_type=jnp.float32)
        + out_bias
    )
    normed_two = layer_norm(after_attn, gain_two, shift_two).astype(jnp.bfloat16)
    pre_act = contract_last(normed_two, up_part) + up_bias
    activated = gelu_tanh(pre_act).astype(jnp.bfloat16)
    result = (
        after_attn + jnp.dot(activated, down_part, preferred_element_type=jnp.float32) + down_bias
    )
    saved_acts = (
        hidden,
        normed_one,
        query_heads,
        key_heads,
        value_heads,
        log_total,
        context,
        after_attn,
        normed_two,
        pre_act,
        activated,
    )
    return (result, saved_acts)


def backward_layer(upstream, params, saved_acts, allowed):
    attn_part, up_part, down_part, vector_part = params
    (
        hidden,
        normed_one,
        query_heads,
        key_heads,
        value_heads,
        log_total,
        context,
        after_attn,
        normed_two,
        pre_act,
        activated,
    ) = saved_acts
    model_width = attn_part.shape[1]
    head_count = model_width // HEAD_DIM
    row_count = hidden.shape[0]
    (
        gain_one,
        shift_one,
        query_bias,
        value_bias,
        out_bias,
        gain_two,
        shift_two,
        down_bias,
        up_bias,
    ) = split_vectors(vector_part, model_width)
    upstream_bf = upstream.astype(jnp.bfloat16)
    grad_down_bias = jnp.sum(upstream, axis=0)
    grad_act = contract_last(upstream_bf, down_part)
    grad_pre = jax.vjp(gelu_tanh, pre_act)[1](grad_act)[0]
    grad_up_bias = jnp.sum(grad_pre, axis=0)
    grad_pre_bf = grad_pre.astype(jnp.bfloat16)
    grad_normed_two = jnp.dot(grad_pre_bf, up_part, preferred_element_type=jnp.float32)
    back_two = jax.vjp(layer_norm, after_attn, gain_two, shift_two)[1]
    grad_mid, grad_gain_two, grad_shift_two = back_two(grad_normed_two)
    grad_mid = upstream + grad_mid
    grad_out_bias = jnp.sum(grad_mid, axis=0)
    grad_mid_bf = grad_mid.astype(jnp.bfloat16)
    grad_context = (
        contract_last(grad_mid_bf, attn_part[3 * model_width :])
        .astype(jnp.bfloat16)
        .reshape(row_count, head_count, HEAD_DIM)
    )
    scores = jnp.where(allowed[None], head_product("qhc,khc->hqk", query_heads, key_heads), -1e30)
    probs_f32 = jnp.exp(scores - log_total[..., None])
    probs_bf = probs_f32.astype(jnp.bfloat16)
    grad_values = head_product("hqk,qhc->khc", probs_bf, grad_context).reshape(
        row_count, model_width
    )
    grad_probs = head_product("qhc,khc->hqk", grad_context, value_heads)
    row_dot = jnp.sum(probs_f32 * grad_probs, axis=-1, keepdims=True)
    grad_scores = (probs_f32 * (grad_probs - row_dot)).astype(jnp.bfloat16)
    grad_query = head_product("hqk,khc->qhc", grad_scores, key_heads).reshape(
        row_count, model_width
    ) * HEAD_DIM ** (-0.5)
    grad_keys = head_product("hqk,qhc->khc", grad_scores, query_heads).reshape(
        row_count, model_width
    )
    grad_query_bias = jnp.sum(grad_query, axis=0)
    grad_value_bias = jnp.sum(grad_values, axis=0)
    grad_proj = jnp.concatenate([grad_query, grad_keys, grad_values], axis=1).astype(jnp.bfloat16)
    grad_normed_one = jnp.dot(
        grad_proj, attn_part[: 3 * model_width], preferred_element_type=jnp.float32
    )
    back_one = jax.vjp(layer_norm, hidden, gain_one, shift_one)[1]
    grad_below, grad_gain_one, grad_shift_one = back_one(grad_normed_one)
    grad_below = grad_mid + grad_below
    left_all = jnp.concatenate([grad_proj, context], axis=1)
    grad_vector = jnp.concatenate(
        [
            grad_gain_one,
            grad_shift_one,
            grad_query_bias,
            grad_value_bias,
            grad_out_bias,
            grad_gain_two,
            grad_shift_two,
            grad_down_bias,
            grad_up_bias,
        ]
    )
    operands = (left_all, normed_one, grad_mid_bf, grad_pre_bf, normed_two, activated, upstream_bf)
    return (grad_below, operands, grad_vector)


def shards(tokens, seq_ends, attn_weight, up_weight, down_weight, vectors, cotangent):
    allowed = causal_mask(seq_ends[0], tokens.shape[0])
    model_width = tokens.shape[1]
    attn_rows = attn_weight.shape[1]
    layer_count = attn_weight.shape[0]
    hidden = tokens.astype(jnp.float32)
    kept_params = []
    layer_idx = 0
    gathered = (
        lax.all_gather(attn_weight[layer_idx], ("dp", "shard"), axis=0, tiled=True),
        lax.all_gather(up_weight[layer_idx], ("dp", "shard"), axis=0, tiled=True),
        lax.all_gather(down_weight[layer_idx], ("dp", "shard"), axis=0, tiled=True),
        lax.all_gather(vectors[layer_idx], ("dp", "shard"), axis=0, tiled=True),
    )
    kept_params.append(gathered)
    hidden, saved_acts = forward_layer(hidden, gathered, allowed)
    saved_list = [saved_acts]
    output = hidden.astype(jnp.bfloat16)
    upstream = cotangent.astype(jnp.float32)
    grad_sets = [None] * layer_count
    for layer_idx in reversed(range(layer_count)):
        gathered = (
            lax.all_gather(attn_weight[layer_idx], ("dp", "shard"), axis=0, tiled=True),
            lax.all_gather(up_weight[layer_idx], ("dp", "shard"), axis=0, tiled=True),
            lax.all_gather(down_weight[layer_idx], ("dp", "shard"), axis=0, tiled=True),
            lax.all_gather(vectors[layer_idx], ("dp", "shard"), axis=0, tiled=True),
        )
        upstream, operands, grad_vector = backward_layer(
            upstream, gathered, saved_list[layer_idx], allowed
        )
        left_all, normed_one, grad_mid_bf, grad_pre_bf, normed_two, activated, upstream_bf = (
            operands
        )
        row_index = jnp.arange(attn_rows * lax.axis_size(("dp", "shard")), dtype=jnp.int32)
        first_rows = jnp.where(
            (row_index < 3 * model_width)[None, :], left_all, jnp.zeros_like(left_all)
        )
        second_rows = jnp.where(
            (row_index >= 3 * model_width)[None, :], left_all, jnp.zeros_like(left_all)
        )
        grad_attn_w = lax.psum_scatter(
            contract_first(first_rows, normed_one) + contract_first(second_rows, grad_mid_bf),
            ("dp", "shard"),
            scatter_dimension=0,
            tiled=True,
        )
        grad_up_w = lax.psum_scatter(
            contract_first(grad_pre_bf, normed_two),
            ("dp", "shard"),
            scatter_dimension=0,
            tiled=True,
        )
        grad_down_w = lax.psum_scatter(
            contract_first(activated, upstream_bf), ("dp", "shard"), scatter_dimension=0, tiled=True
        )
        grad_vec_own = lax.psum_scatter(
            grad_vector, ("dp", "shard"), scatter_dimension=0, tiled=True
        )
        grad_sets[layer_idx] = (grad_attn_w, grad_up_w, grad_down_w, grad_vec_own)
    grad_attn = jnp.stack([grad_sets[0][0]])
    grad_up = jnp.stack([grad_sets[0][1]])
    grad_down = jnp.stack([grad_sets[0][2]])
    grad_vectors = jnp.stack([grad_sets[0][3]])
    return (output, upstream, grad_attn, grad_up, grad_down, grad_vectors)


def solution(mesh):
    return jax.shard_map(
        shards,
        mesh=mesh,
        in_specs=(
            P(("dp", "shard"), None),
            P(("dp", "shard"), None),
            P(None, ("dp", "shard"), None),
            P(None, ("dp", "shard"), None),
            P(None, ("dp", "shard"), None),
            P(None, ("dp", "shard")),
            P(("dp", "shard"), None),
        ),
        out_specs=(
            P(("dp", "shard"), None),
            P(("dp", "shard"), None),
            P(None, ("dp", "shard"), None),
            P(None, ("dp", "shard"), None),
            P(None, ("dp", "shard"), None),
            P(None, ("dp", "shard")),
        ),
        check_vma=False,
    )
```

profile of v0, /device:TPU:0, one launch (start us, length us, event | category | flops | bytes accessed | tf_op | source)
XLA Modules:
  0.0 987.9 jit_solution(13790586589980789792)
XLA Ops:
  7.9 0.7 all-gather.10.cloned.1.call-update
  8.7 0.7 all-gather.12.cloned.1.call-update
  9.4 0.7 reduce.3
  10.4 43.7 %all-reduce = bf16[13056]{0:T(1024)(128)(2,1)S(1)} all-reduce(bf16[13056]{0:T(1024)(128)(2,1)S(1)} %dynamic-update-slice), channel_id=2, replica_groups=mesh['dp'=16,'shard'=2] {'dp','shard'}, use_global_device_ids=true, to_apply=%add | all-reduce | flops 13056 | bytes 52224
  54.2 0.7 convert_reduce_fusion.2
  55.1 1.1 convert_reduce_fusion
  56.2 1.1 fusion.54
  57.4 40.9 %all-gather.8.cloned.1.call-done = bf16[1,4352,1088]{2,1,0:T(8,128)(2,1)} async-done(((bf16[1,136,1088]{2,1,0:T(8,128)(2,1)}), bf16[1,4352,1088]{2,1,0:T(8,128)(2,1)}) %all-gather.8.cloned.1.call-update) | async-done | bytes 9469968 | tf_op jit(solution)/shard_map/all_gather | solution.py:220
  98.4 5.4 fusion.10
  105.2 3.0 fusion.94
  108.3 75.5 %all-gather.10.cloned.1.call-done = bf16[1,4352,1088]{2,1,0:T(8,128)(2,1)} async-done(((bf16[1,136,1088]{2,1,0:T(8,128)(2,1)}), bf16[1,4352,1088]{2,1,0:T(8,128)(2,1)}) %all-gather.10.cloned.1.call-update) | async-done | bytes 9469968 | tf_op jit(solution)/shard_map/all_gather | solution.py:221
  183.9 7.2 fusion.11
  191.1 78.3 %all-gather.12.cloned.1.call-done = bf16[1,4352,1088]{2,1,0:T(8,128)(2,1)} async-done(((bf16[1,136,1088]{2,1,0:T(8,128)(2,1)}), bf16[1,4352,1088]{2,1,0:T(8,128)(2,1)}) %all-gather.12.cloned.1.call-update) | async-done | bytes 9469968 | tf_op jit(solution)/shard_map/all_gather | solution.py:222
  269.4 7.4 fusion.97
  276.8 4.7 multiply_reduce_fusion.1
  281.9 0.8 copy-done.2
  282.8 3.3 convolution_convert_fusion
  286.1 3.0 fusion.92
  289.1 1.4 fusion.98
  290.5 1.3 multiply_reduce_fusion
  292.1 0.7 copy-done.9
  293.7 14.5 %fusion.35 = f32[4352,1088]{1,0:T(8,128)} fusion(pred[4352]{0:T(1024)(128)(4,1)S(1)} %iota_compare_fusion.2, bf16[128,1088]{0,1:T(8,128)(2,1)S(1)} %bitcast.88, bf16[128,1088]{0,1:T(8,128)(2,1)S(1)} %bitcast.85, bf16[128,1088]{0,1:T(8,128)(2,1)S(1)} %bitcast.74, bf16[128,1088]{0,1:T(8,128)(2,1)S(1)} %bitcast.77, bf16[128,1088]{0,1:T(8,128)(2,1)S(1)} %copy-done.1, ...), kind=kOutput, calls=%fused_computation.41 | convolution fusion | flops 1218002944 | bytes 20346624 | tf_op jit(solution)/shard_map/dot_general | solution.py:32
  308.2 20.0 %convolution_add_fusion = f32[4352,1088]{1,0:T(8,128)} fusion(f32[4352,1088]{1,0:T(8,128)} %fusion.35, bf16[128,1088]{0,1:T(8,128)(2,1)S(1)} %copy-done.18, pred[4352]{0:T(1024)(128)(4,1)S(1)} %iota_compare_fusion.1, bf16[128,1088]{0,1:T(8,128)(2,1)S(1)} %bitcast.89, bf16[128,1088]{0,1:T(8,128)(2,1)S(1)} %bitcast.86, bf16[128,1088]{0,1:T(8,128)(2,1)S(1)} %bitcast.75, ...), kind=kOutput, calls=%fused_computation.1 | convolution fusion | flops 1221902336 | bytes 39276800 | tf_op jit(solution)/shard_map/dot_general | solution.py:32
  328.2 12.6 %fusion.61 = f32[4352,1088]{1,0:T(8,128)} fusion(bf16[128,4352]{1,0:T(8,128)(2,1)} %copy-done.4, f32[128,1088]{0,1:T(8,128)S(1)} %get-tuple-element.33, f32[1088]{0:T(1024)S(1)} %get-tuple-element.16, f32[1088]{0:T(1024)S(1)} %get-tuple-element.15, f32[128]{0:T(128)S(1)} %fusion.81, f32[128]{0:T(128)S(1)} %broadcast_multiply_fusion), kind=kOutput, calls=%fused_computation.82 | convolution fusion | flops 1212850176 | bytes 20620800 | tf_op jit(solution)/shard_map/dot_general | solution.py:32
  340.9 11.0 %fusion.89 = f32[4352,1088]{1,0:T(8,128)} fusion(bf16[128,1088]{0,1:T(8,128)(2,1)} %param.13, f32[128,4352]{1,0:T(8,128)S(1)} %fusion.11), kind=kOutput, calls=%fused_computation.124 | convolution fusion | flops 1217167360 | bytes 21446656 | tf_op jit(solution)/shard_map/dot_general | solution.py:32
  352.1 7.2 fusion.90
  359.8 1.2 convert_reduce_fusion.1
  361.1 40.9 %all-reduce.4 = f32[13056]{0:T(1024)S(1)} all-reduce(f32[13056]{0:T(1024)S(1)} %concatenate.13), channel_id=9, replica_groups=mesh['dp'=16,'shard'=2] {'dp','shard'}, use_global_device_ids=true, to_apply=%region_23.24.clone | all-reduce | flops 13056 | bytes 104448
  402.6 8.3 fusion.21
  411.0 130.0 %reduce-scatter.10.cloned.1.call-done = f32[136,1088]{1,0:T(8,128)} async-done(((f32[4352,1088]{1,0:T(8,128)}), f32[136,1088]{1,0:T(8,128)}) %reduce-scatter.10.cloned.1.call-update) | async-done | bytes 591888
  540.9 219.9 %reduce-scatter.12.cloned.1.call-done = f32[136,1088]{1,0:T(8,128)} async-done(((f32[4352,1088]{1,0:T(8,128)}), f32[136,1088]{1,0:T(8,128)}) %reduce-scatter.12.cloned.1.call-update) | async-done | bytes 591888
  760.9 219.9 %reduce-scatter.14.cloned.1.call-done = f32[136,1088]{1,0:T(8,128)} async-done(((f32[4352,1088]{1,0:T(8,128)}), f32[136,1088]{1,0:T(8,128)}) %reduce-scatter.14.cloned.1.call-update) | async-done | bytes 591888
  (81 shorter events, 5.7 us)
Async XLA Ops:
  7.2 91.2 %all-gather.8.cloned.1.call-start = ((), (), s32[]{:S(2)}) async-start(), calls=%async_computation.3 | async-start | bytes 10340352 | tf_op jit(solution)/shard_map/all_gather | solution.py:220
  7.9 176.0 %all-gather.10.cloned.1.call-start = ((), (), s32[]{:S(2)}) async-start(), calls=%async_computation.4 | async-start | bytes 10340352 | tf_op jit(solution)/shard_map/all_gather | solution.py:221
  8.6 260.7 %all-gather.12.cloned.1.call-start = ((), (), s32[]{:S(2)}) async-start(), calls=%async_computation.5 | async-start | bytes 10340352 | tf_op jit(solution)/shard_map/all_gather | solution.py:222
  9.4 531.5 %reduce-scatter.10.cloned.1.call-start = ((), (), s32[]{:S(2)}) async-start(), calls=%async_computation.6 | async-start | bytes 20680704
  103.9 1.3 copy-start.10
  103.9 1.3 copy-start.1
  104.2 0.9 copy-start.8
  104.3 3.9 copy-start.19
  104.6 3.5 copy-start.5
  105.1 3.2 copy-start.15
  183.9 85.5 %copy-start.12 = (bf16[128,1088]{0,1:T(8,128)(2,1)S(1)}, bf16[128,1088]{0,1:T(8,128)(2,1)}, u32[]{:S(2)}) copy-start(bf16[128,1088]{0,1:T(8,128)(2,1)} %param.13) | copy-start | bytes 835588
  269.4 7.5 copy-start
  276.8 4.8 copy-start.4
  281.8 0.8 copy-start.2
  282.7 3.4 copy-start.17
  282.7 6.4 copy-start.20
  289.1 1.4 copy-start.6
  291.9 1.0 copy-start.9
  291.9 1.4 copy-start.11
  291.9 1.8 copy-start.14
  291.9 1.8 copy-start.16
  293.7 14.5 %copy-start.7 = (bf16[17,64,128]{2,1,0:T(8,128)(2,1)}, bf16[17,64,128]{2,1,0:T(8,128)(2,1)S(1)}, u32[]{:S(2)}) copy-start(bf16[17,64,128]{2,1,0:T(8,128)(2,1)S(1)} %get-tuple-element.31) | copy-start | bytes 835588
  293.7 14.5 %copy-start.18 = (bf16[128,1088]{0,1:T(8,128)(2,1)S(1)}, bf16[128,1088]{0,1:T(8,128)(2,1)}, u32[]{:S(2)}) copy-start(bf16[128,1088]{0,1:T(8,128)(2,1)} %copy-done.17) | copy-start | bytes 835588
  328.2 432.7 %reduce-scatter.12.cloned.1.call-start = ((), (), s32[]{:S(2)}) async-start(), calls=%async_computation.7 | async-start | bytes 20680704
  340.8 639.9 %reduce-scatter.14.cloned.1.call-start = ((), (), s32[]{:S(2)}) async-start(), calls=%async_computation.8 | async-start | bytes 20680704
  352.1 7.7 copy-start.3
  352.1 7.7 copy-start.13
Sparse Core Ops, SparseCore 0:
  10.8 87.5 all-gather.7
  101.2 82.5 all-gather.9
  186.7 82.5 all-gather.11
  328.3 212.5 reduce-scatter.9
  547.8 213.0 reduce-scatter.11
  767.7 213.0 reduce-scatter.13
where the time goes:
time: 998 us; the launch traced here: 988 us
  waiting for transfers between devices  767 us (77%)
  matrix products  111 us (11%)
  blocking collectives  84.6 us (8%)
  between operations  14.8 us (1%)
    unnamed x9, waiting for transfers between devices  572 us
    unnamed x2, blocking collectives  84.6 us
    all_gather x1, waiting for transfers between devices, shards(): lax.all_gather(down_weight[layer_idx], ('dp', 'shard'), axis=0, tiled=True)  78.3 us
    all_gather x1, waiting for transfers between devices, shards(): lax.all_gather(up_weight[layer_idx], ('dp', 'shard'), axis=0, tiled=True)  75.5 us
    dot_general x4, matrix products, contract_first(): lax.dot_general(left, right, (((0,), (0,)), ((), ())), preferred_element_...  58 us
    all_gather x1, waiting for transfers between devices, shards(): lax.all_gather(attn_weight[layer_idx], ('dp', 'shard'), axis=0, tiled=True)  40.9 us
    dot_general x4, matrix products, contract_last(): lax.dot_general(left, right, (((1,), (1,)), ((), ())), preferred_element_...  23.5 us
  transfers between devices with their start and end apart: 6, of which 6 were waited for; matrix products, arithmetic and copies ran while one was open for 6% of the time, Pallas kernels for 0%

commit v1 on v0

--- a/solution.py
+++ b/solution.py
@@ -5,6 +5,26 @@
 
 HEAD_DIM = 64
 EPS = 1e-05
+
+
+def perform_the_spans(array_in, axis_k):
+    tile_out = list(array_in.shape[1:])
+    tile_out[axis_k] *= array_in.shape[0]
+    found_now = jnp.moveaxis(array_in, 0, axis_k).reshape(tile_out)
+    return found_now
+
+
+def set_start(x0, link_axis):
+    total_devices = lax.axis_size(link_axis)
+    ready = x0[None]
+    for pp in range(total_devices.bit_length() - 1):
+        low = 1 << pp
+        e_next = tuple(((q, q ^ low) for q in range(total_devices)))
+        mixed_arr = lax.ppermute(ready, axis_name=link_axis, perm=e_next)
+        left_arr = jnp.stack([ready, mixed_arr], axis=0)
+        then = lax.axis_index(link_axis) >> pp & 1
+        ready = jnp.where(then == 0, left_arr, left_arr[::-1]).reshape(-1, *x0.shape)
+    return ready
 
 
 def layer_norm(values, gain, shift):
@@ -209,6 +229,12 @@
 
 
 def shards(tokens, seq_ends, attn_weight, up_weight, down_weight, vectors, cotangent):
+
+    def serve_rates_in(row_data, t0, row_dim):
+        fresh = set_start(row_data, t0)
+        arr_out = perform_the_spans(fresh, row_dim)
+        return arr_out
+
     allowed = causal_mask(seq_ends[0], tokens.shape[0])
     model_width = tokens.shape[1]
     attn_rows = attn_weight.shape[1]
@@ -219,7 +245,7 @@
     gathered = (
         lax.all_gather(attn_weight[layer_idx], ("dp", "shard"), axis=0, tiled=True),
         lax.all_gather(up_weight[layer_idx], ("dp", "shard"), axis=0, tiled=True),
-        lax.all_gather(down_weight[layer_idx], ("dp", "shard"), axis=0, tiled=True),
+        serve_rates_in(down_weight[layer_idx], ("dp", "shard"), 0),
         lax.all_gather(vectors[layer_idx], ("dp", "shard"), axis=0, tiled=True),
     )
     kept_params.append(gathered)

time: 998 us -> 1220 us (1.22)
  waiting for transfers between devices: 767 us -> 954 us
  other arithmetic: 7.82 us -> 37.5 us
    ppermute x0 -> x5, waiting for transfers between devices: none -> 396 us  [set_start(): mixed_arr = lax.ppermute(ready, axis_name=link_axis, perm=e_next)]
    unnamed x9, waiting for transfers between devices: 572 us -> 364 us
    select_n x0 -> x4, other arithmetic: none -> 17.9 us  [set_start(): jnp.where(then == 0, left_arr, left_arr[::-1]).reshape(-1, *x0.shape)]
  transfers between devices with their start and end apart: 6 -> 11, of which waited for: 6 -> 10; matrix products, arithmetic and copies ran while one was open for 6% -> 8% of each run, Pallas kernels for 0% -> 0%
where the time goes in v1:
time: 1220 us; the launch traced here: 1210 us
  waiting for transfers between devices  954 us (78%)
  matrix products  104 us (9%)
  blocking collectives  82.8 us (7%)
  other arithmetic  37.5 us (3%)
  between operations  15.1 us (1%)
    ppermute x5, waiting for transfers between devices, set_start(): mixed_arr = lax.ppermute(ready, axis_name=link_axis, perm=e_next)  396 us
    unnamed x9, waiting for transfers between devices  364 us
    unnamed x2, blocking collectives  82.8 us
    all_gather x1, waiting for transfers between devices, shards(): lax.all_gather(down_weight[layer_idx], ('dp', 'shard'), axis=0, tiled=True)  78.2 us
    all_gather x1, waiting for transfers between devices, shards(): lax.all_gather(up_weight[layer_idx], ('dp', 'shard'), axis=0, tiled=True)  75.5 us
    dot_general x4, matrix products, contract_first(): lax.dot_general(left, right, (((0,), (0,)), ((), ())), preferred_element_...  53.5 us
    all_gather x1, waiting for transfers between devices, shards(): lax.all_gather(attn_weight[layer_idx], ('dp', 'shard'), axis=0, tiled=True)  40.9 us
  transfers between devices with their start and end apart: 11, of which 10 were waited for; matrix products, arithmetic and copies ran while one was open for 8% of the time, Pallas kernels for 0%

profile of v1, /device:TPU:0, one launch (start us, length us, event | category | flops | bytes accessed | tf_op | source)
XLA Modules:
  0.0 1207.4 jit_solution(80014468825780379)
XLA Ops:
  10.4 43.7 %all-reduce = bf16[13056]{0:T(1024)(128)(2,1)S(1)} all-reduce(bf16[13056]{0:T(1024)(128)(2,1)S(1)} %dynamic-update-slice), channel_id=2, replica_groups=mesh['dp'=16,'shard'=2] {'dp','shard'}, use_global_device_ids=true, to_apply=%add | all-reduce | flops 13056 | bytes 52224
  57.4 40.9 %all-gather.8.cloned.1.call-done = bf16[1,4352,1088]{2,1,0:T(8,128)(2,1)} async-done(((bf16[1,136,1088]{2,1,0:T(8,128)(2,1)}), bf16[1,4352,1088]{2,1,0:T(8,128)(2,1)}) %all-gather.8.cloned.1.call-update) | async-done | bytes 9469968 | tf_op jit(solution)/shard_map/all_gather | solution.py:246
  98.4 5.4 fusion.8
  105.2 3.0 fusion.87
  108.3 75.5 %all-gather.10.cloned.1.call-done = bf16[1,4352,1088]{2,1,0:T(8,128)(2,1)} async-done(((bf16[1,136,1088]{2,1,0:T(8,128)(2,1)}), bf16[1,4352,1088]{2,1,0:T(8,128)(2,1)}) %all-gather.10.cloned.1.call-update) | async-done | bytes 9469968 | tf_op jit(solution)/shard_map/all_gather | solution.py:247
  183.9 7.2 fusion.9
  191.1 78.2 %all-gather.12.cloned.1.call-done = bf16[1,4352,1088]{2,1,0:T(8,128)(2,1)} async-done(((bf16[1,136,1088]{2,1,0:T(8,128)(2,1)}), bf16[1,4352,1088]{2,1,0:T(8,128)(2,1)}) %all-gather.12.cloned.1.call-update) | async-done | bytes 9469968 | tf_op jit(solution)/shard_map/all_gather | solution.py:261
  269.4 7.4 fusion.90
  276.8 4.5 multiply_reduce_fusion.1
  283.1 2.6 convolution_convert_fusion
  290.9 2.9 fusion.85
  293.8 11.0 fusion.26
  304.9 20.0 %convolution_add_fusion = f32[4352,1088]{1,0:T(8,128)} fusion(f32[4352,1088]{1,0:T(8,128)} %fusion.26, bf16[128,1088]{0,1:T(8,128)(2,1)S(1)} %copy-done.26, pred[4352]{0:T(1024)(128)(4,1)S(1)} %iota_compare_fusion.1, bf16[128,1088]{0,1:T(8,128)(2,1)S(1)} %bitcast.106, bf16[128,1088]{0,1:T(8,128)(2,1)S(1)} %bitcast.102, bf16[128,1088]{0,1:T(8,128)(2,1)S(1)} %bitcast.93, ...), kind=kOutput, calls=%fused_computation.1 | convolution fusion | flops 1221902336 | bytes 39276800 | tf_op jit(solution)/shard_map/dot_general | solution.py:52
  324.9 12.6 %fusion.52 = f32[4352,1088]{1,0:T(8,128)} fusion(bf16[128,4352]{1,0:T(8,128)(2,1)} %copy-done.6, f32[128,1088]{0,1:T(8,128)S(1)} %get-tuple-element.35, f32[1088]{0:T(1024)S(1)} %get-tuple-element.16, f32[1088]{0:T(1024)S(1)} %get-tuple-element.15, f32[128]{0:T(128)S(1)} %fusion.74, f32[128]{0:T(128)S(1)} %broadcast_multiply_fusion), kind=kOutput, calls=%fused_computation.90 | convolution fusion | flops 1212850176 | bytes 20620800 | tf_op jit(solution)/shard_map/dot_general | solution.py:52
  338.5 10.0 fusion.82
  349.5 1.5 collective-permute-start
  351.0 8.1 collective-permute-done
  359.4 2.3 collective-permute-done.1
  362.0 1.6 collective-permute-start.2
  363.6 34.5 %collective-permute-done.2 = bf16[4,136,1088]{2,1,0:T(8,128)(2,1)S(1)} collective-permute-done((bf16[4,136,1088]{2,1,0:T(8,128)(2,1)S(1)}, bf16[4,136,1088]{2,1,0:T(8,128)(2,1)S(1)}, u32[]{:S(2)}, u32[]{:S(2)}) %collective-permute-start.2) | collective-permute-done | bytes 1183776 | tf_op jit(solution)/shard_map/ppermute | solution.py:23
  400.3 94.7 %collective-permute-done.3 = bf16[8,136,1088]{2,1,0:T(8,128)(2,1)} collective-permute-done((bf16[8,136,1088]{2,1,0:T(8,128)(2,1)S(1)}, bf16[8,136,1088]{2,1,0:T(8,128)(2,1)}, u32[]{:S(2)}, u32[]{:S(2)}) %collective-permute-start.3) | collective-permute-done | bytes 2367520 | tf_op jit(solution)/shard_map/ppermute | solution.py:23
  495.0 2.3 pad_maximum_fusion.1
  497.3 3.1 reverse_select_fusion.1
  500.4 1.7 collective-permute-start.4
  502.0 256.1 %collective-permute-done.4 = bf16[16,136,1088]{2,1,0:T(8,128)(2,1)} collective-permute-done((bf16[16,136,1088]{2,1,0:T(8,128)(2,1)}, bf16[16,136,1088]{2,1,0:T(8,128)(2,1)}, u32[]{:S(2)}, u32[]{:S(2)}) %collective-permute-start.4) | collective-permute-done | bytes 4735008 | tf_op jit(solution)/shard_map/ppermute | solution.py:23
  758.1 8.9 pad_maximum_fusion
  767.0 14.1 %reverse_select_fusion = bf16[2,16,136,1088]{3,2,1,0:T(8,128)(2,1)} fusion(bf16[2,16,136,1088]{3,2,1,0:T(8,128)(2,1)} %pad_maximum_fusion, pred[]{:T(512)S(6)} %eq.35), kind=kLoop, calls=%fused_computation.2 | loop fusion | flops 4734976 | bytes 18939904 | tf_op jit(solution)/shard_map/jit(_where)/select_n | solution.py:26
  781.3 7.0 fusion.83
  790.1 39.1 %all-reduce.4 = f32[13056]{0:T(1024)S(1)} all-reduce(f32[13056]{0:T(1024)S(1)} %concatenate.13), channel_id=9, replica_groups=mesh['dp'=16,'shard'=2] {'dp','shard'}, use_global_device_ids=true, to_apply=%region_23.24.clone | all-reduce | flops 13056 | bytes 104448
  829.9 8.1 fusion.14
  838.0 142.0 %reduce-scatter.12.cloned.1.call-done = f32[136,1088]{1,0:T(8,128)} async-done(((f32[4352,1088]{1,0:T(8,128)}), f32[136,1088]{1,0:T(8,128)}) %reduce-scatter.12.cloned.1.call-update) | async-done | bytes 591888
  980.0 220.0 %reduce-scatter.14.cloned.1.call-done = f32[136,1088]{1,0:T(8,128)} async-done(((f32[4352,1088]{1,0:T(8,128)}), f32[136,1088]{1,0:T(8,128)}) %reduce-scatter.14.cloned.1.call-update) | async-done | bytes 591888
  (119 shorter events, 22.3 us)
Async XLA Ops:
  7.2 91.2 %all-gather.8.cloned.1.call-start = ((), (), s32[]{:S(2)}) async-start(), calls=%async_computation.3 | async-start | bytes 10340352 | tf_op jit(solution)/shard_map/all_gather | solution.py:246
  7.9 176.0 %all-gather.10.cloned.1.call-start = ((), (), s32[]{:S(2)}) async-start(), calls=%async_computation.4 | async-start | bytes 10340352 | tf_op jit(solution)/shard_map/all_gather | solution.py:247
  8.6 260.7 %all-gather.12.cloned.1.call-start = ((), (), s32[]{:S(2)}) async-start(), calls=%async_computation.5 | async-start | bytes 10340352 | tf_op jit(solution)/shard_map/all_gather | solution.py:261
  9.4 828.7 %reduce-scatter.10.cloned.1.call-start = ((), (), s32[]{:S(2)}) async-start(), calls=%async_computation.6 | async-start | bytes 20680704
  104.3 3.9 copy-start.27
  104.6 3.5 copy-start.7
  105.1 3.2 copy-start.23
  183.9 85.5 %copy-start.17 = (bf16[128,1088]{0,1:T(8,128)(2,1)S(1)}, bf16[128,1088]{0,1:T(8,128)(2,1)}, u32[]{:S(2)}) copy-start(bf16[128,1088]{0,1:T(8,128)(2,1)} %param.13) | copy-start | bytes 835588
  191.1 146.5 %copy-start.1 = (f32[128,4352]{1,0:T(8,128)}, f32[128,4352]{1,0:T(8,128)S(1)}, u32[]{:S(2)}) copy-start(f32[128,4352]{1,0:T(8,128)S(1)} %fusion.9) | copy-start | bytes 6684676
  269.4 7.5 copy-start
  276.8 4.5 copy-start.6
  283.1 2.6 copy-start.28
  285.7 2.6 copy-start.29
  285.7 1.4 copy-start.8
  289.7 15.1 %copy-start.9 = (bf16[17,64,128]{2,1,0:T(8,128)(2,1)}, bf16[17,64,128]{2,1,0:T(8,128)(2,1)S(1)}, u32[]{:S(2)}) copy-start(bf16[17,64,128]{2,1,0:T(8,128)(2,1)S(1)} %get-tuple-element.33) | copy-start | bytes 835588
  293.8 11.0 copy-start.11
  293.8 11.0 copy-start.21
  293.8 11.0 copy-start.24
  293.8 11.0 copy-start.26
  324.9 655.1 %reduce-scatter.12.cloned.1.call-start = ((), (), s32[]{:S(2)}) async-start(), calls=%async_computation.7 | async-start | bytes 20680704
  337.6 862.5 %reduce-scatter.14.cloned.1.call-start = ((), (), s32[]{:S(2)}) async-start(), calls=%async_computation.8 | async-start | bytes 20680704
  349.5 9.6 collective-permute-start
  359.3 2.4 collective-permute-start.1
  362.0 36.1 %collective-permute-start.2 = (bf16[4,136,1088]{2,1,0:T(8,128)(2,1)S(1)}, bf16[4,136,1088]{2,1,0:T(8,128)(2,1)S(1)}, u32[]{:S(2)}, u32[]{:S(2)}) collective-permute-start(bf16[4,136,1088]{2,1,0:T(8,128)(2,1)S(1)} %bitcast.87), channel_id=1, source_target_pairs={{0,4},{1,5},{2,6},{3,7},{4,0},{5,1},{6,2},{7,3},{8,12},{9,13},{10,... | collective-permute-start | bytes 3551240 | tf_op jit(solution)/shard_map/ppermute | solution.py:23
  398.9 96.0 %collective-permute-start.3 = (bf16[8,136,1088]{2,1,0:T(8,128)(2,1)S(1)}, bf16[8,136,1088]{2,1,0:T(8,128)(2,1)}, u32[]{:S(2)}, u32[]{:S(2)}) collective-permute-start(bf16[8,136,1088]{2,1,0:T(8,128)(2,1)S(1)} %bitcast.85), channel_id=1, source_target_pairs={{0,8},{1,9},{2,10},{3,11},{4,12},{5,13},{6,14},{7,15},{8,0},{9,1},... | collective-permute-start | bytes 7102472 | tf_op jit(solution)/shard_map/ppermute | solution.py:23
  500.4 257.8 %collective-permute-start.4 = (bf16[16,136,1088]{2,1,0:T(8,128)(2,1)}, bf16[16,136,1088]{2,1,0:T(8,128)(2,1)}, u32[]{:S(2)}, u32[]{:S(2)}) collective-permute-start(bf16[16,136,1088]{2,1,0:T(8,128)(2,1)} %bitcast.21), channel_id=1, source_target_pairs={{0,16},{1,17},{2,18},{3,19},{4,20},{5,21},{6,22},{7,23},{8,24},{9,... | collective-permute-start | bytes 14204936 | tf_op jit(solution)/shard_map/ppermute | solution.py:23
  767.0 14.2 %copy-start.10 = (bf16[17,64,128]{2,1,0:T(8,128)(2,1)S(1)}, bf16[17,64,128]{2,1,0:T(8,128)(2,1)}, u32[]{:S(2)}) copy-start(bf16[17,64,128]{2,1,0:T(8,128)(2,1)} %copy-done.9) | copy-start | bytes 835588
  767.0 14.2 %copy-start.12 = (bf16[17,64,128]{2,1,0:T(8,128)(2,1)S(1)}, bf16[17,64,128]{2,1,0:T(8,128)(2,1)}, u32[]{:S(2)}) copy-start(bf16[17,64,128]{2,1,0:T(8,128)(2,1)} %convolution_convert_fusion.1) | copy-start | bytes 835588
  767.0 14.2 %copy-start.22 = (bf16[128,17,64]{0,2,1:T(8,128)(2,1)S(1)}, bf16[128,17,64]{0,2,1:T(8,128)(2,1)}, u32[]{:S(2)}) copy-start(bf16[128,17,64]{0,2,1:T(8,128)(2,1)} %get-tuple-element.31) | copy-start | bytes 835588
  781.3 7.5 copy-start.5
  781.3 7.5 copy-start.19
  788.3 41.6 %copy-start.2 = (f32[128,4352]{1,0:T(8,128)S(1)}, f32[128,4352]{1,0:T(8,128)}, u32[]{:S(2)}) copy-start(f32[128,4352]{1,0:T(8,128)} %copy-done.1) | copy-start | bytes 6684676
  (9 other events, 9.2 us)
Sparse Core Ops, SparseCore 0:
  10.8 87.5 all-gather.7
  101.2 82.5 all-gather.9
  186.7 82.5 all-gather.11
  325.0 367.1 reduce-scatter.9
  699.1 280.9 reduce-scatter.11
  986.9 213.1 reduce-scatter.13
